TPU v7x, 32 devices: a whole 2x2x4 slice. The times are simulated.
32 devices in a mesh: region: 2 (over y), member: 8 (over z, core), space: 2 (over x).
Axes of the slice: x: 2, y: 2, z: 4, core: 2. Of those that a mesh axis runs over, the one named last changes fastest.
Arguments:
- prior_trials: bfloat16 [80, 1536, 256], P('member', ('region', 'space')), parts along dimension 1, may hold values from -6 to 6
- prior_at_sensors: bfloat16 [80, 1536], P('member', ('region', 'space')), parts along dimension 1, may hold values from -6 to 6
- sensor_readings: bfloat16 [1536], P(('region', 'space')), parts along dimension 0, may hold values from -8 to 8
- sensor_noise_spread: bfloat16 [1536], P(('region', 'space')), parts along dimension 0, may hold values from 1 to 10
- nearby_readings: int32 [1536, 128], P(('region', 'space')), parts along dimension 0, may hold values from 0 to 1023, as said below
- subarea_cutoff_level: int32 [1536], P(('region', 'space')), parts along dimension 0, may hold values from 0 to 3
Outputs:
- analysis: bfloat16 [80, 1536, 256], P('member', ('region', 'space')), parts along dimension 1
There are 2 independent parts, one for each index of `region`. A program takes and returns all parts, laid end to end along the dimension named above; each array names one. Nothing has to cross between parts.
Inputs may be any that keep to these rules, and one draw needn't show every extreme that they name: `nearby_readings`: row c lists 128 distinct observations whose region-wide index o lies within (subarea_cutoff_level[c] + 2) * 64 of c and inside the region.
All inputs are finite; a program needn't handle non-finite values. Where the computation divides by a largest or mean magnitude, that divisor is 1e-20 or more.
Results may differ from a plain program's by a relative error of at most 0.0053.
Values may be sent and summed in bfloat16 or wider, within the bound.
A program may use at most 64 MiB of HBM per device.

v0:
```python
import jax
import jax.numpy as jnp
from jax import lax
from jax.sharding import PartitionSpec as P

NS_STEPS = 4


def padded(value, sides, width):
    for axis, dim in sides:
        count, length = (lax.axis_size(axis), value.shape[dim])
        up = [(i, (i + 1) % count) for i in range(count - 1)]
        down = [(j, i) for i, j in up]
        last = lax.slice_in_dim(value, length - width, length, axis=dim)
        leading = lax.slice_in_dim(value, 0, width, axis=dim)
        before = lax.ppermute(last, axis, up)
        after = lax.ppermute(leading, axis, down)
        value = jnp.concatenate([before, value, after], axis=dim)
    return value


def prepare(picked, trial_lines, offsets, tier_ids, obs_count):
    observ = picked[:trial_lines]
    ens_mean = jnp.mean(observ, axis=0)
    anomaly = observ - ens_mean
    innovation = picked[trial_lines] - ens_mean
    radius = (tier_ids.astype(jnp.float32) + 2.0) * (0.5 * obs_count)
    distance = jnp.abs(offsets).astype(jnp.float32) / radius[:, None]
    weight = jnp.exp(-2.0 * distance * distance) / picked[trial_lines + 1]
    return (anomaly, innovation, weight)


def spread_terms(anomaly, innovation, weight, trial_lines):
    fit_sum = jnp.sum(weight * innovation * innovation)
    spread = jnp.sum(weight * jnp.sum(anomaly * anomaly, axis=0)) / (trial_lines - 1.0)
    return (fit_sum, spread)


def transform(anomaly, innovation, weight, inflation, trial_lines, sweeps):
    exact = lax.Precision.HIGHEST
    weighted = anomaly * weight[None]
    gram = jnp.einsum("ank,bnk->abn", weighted, anomaly, precision=exact)
    identity = jnp.eye(trial_lines, dtype=jnp.float32)[:, :, None]
    matrix = gram + (trial_lines - 1.0) / inflation * identity
    row_bound = jnp.max(jnp.sum(jnp.abs(matrix), axis=1), axis=0)
    root_iter = matrix / row_bound
    inverse = jnp.broadcast_to(identity, matrix.shape)
    for repeat in range(sweeps):
        factor = 1.5 * identity - 0.5 * jnp.einsum(
            "abn,bcn->acn", inverse, root_iter, precision=exact
        )
        root_iter = jnp.einsum("abn,bcn->acn", root_iter, factor, precision=exact)
        inverse = jnp.einsum("abn,bcn->acn", factor, inverse, precision=exact)
    inv_root = inverse / jnp.sqrt(row_bound)
    target = jnp.sum(weighted * innovation[None], axis=2)
    half_gain = jnp.einsum("abn,bn->an", inv_root, target, precision=exact)
    mean_gain = jnp.einsum("abn,bn->an", inv_root, half_gain, precision=exact)
    weights_full = jnp.sqrt(trial_lines - 1.0) * inv_root + mean_gain[:, None, :]
    centred = weights_full - jnp.mean(weights_full, axis=0, keepdims=True) + 1.0 / trial_lines
    return centred.astype(jnp.bfloat16)


def select_domains(window, trial_lines, obs_lists, col_ids, tier_ids, halo_cells):
    row_count = window.shape[0]
    dom_count, obs_count = obs_lists.shape
    picked = jnp.take(window, obs_lists.reshape(-1), axis=1).reshape(
        row_count, dom_count, obs_count
    )
    picked = picked.astype(jnp.float32)
    offsets = obs_lists - (col_ids + halo_cells)[:, None]
    return prepare(picked, trial_lines, offsets, tier_ids, obs_count)


def per_device(
    prior_trials,
    prior_at_sensors,
    sensor_readings,
    sensor_noise_spread,
    nearby_readings,
    subarea_cutoff_level,
):
    patch_cells = prior_trials.shape[1]
    obs_count = nearby_readings.shape[1]
    halo_cells = 5 * obs_count // 2
    groups = lax.axis_size("member")
    domains = patch_cells // groups
    obs_rows = jnp.stack([sensor_readings, sensor_noise_spread], axis=0)
    gathered = lax.all_gather(prior_at_sensors, "member", axis=0, tiled=True)
    window = padded(jnp.concatenate([gathered, obs_rows], axis=0), (("space", 1),), halo_cells)
    trial_lines = window.shape[0] - 2
    first_col = lax.axis_index("member") * domains
    own_lists = lax.dynamic_slice_in_dim(nearby_readings, first_col, domains, 0)
    own_tiers = lax.dynamic_slice_in_dim(subarea_cutoff_level, first_col, domains, 0)
    own_columns = first_col + jnp.arange(domains, dtype=jnp.int32)
    anomaly, innovation, weight = select_domains(
        window, trial_lines, own_lists, own_columns, own_tiers, halo_cells
    )
    fit_sum, spread = spread_terms(anomaly, innovation, weight, trial_lines)
    fit_sum, spread = lax.psum((fit_sum, spread), ("member", "space"))
    inflation = fit_sum / spread
    trans_w = transform(anomaly, innovation, weight, inflation, trial_lines, NS_STEPS)
    incoming_pieces = lax.all_to_all(
        prior_trials, "member", split_axis=1, concat_axis=0, tiled=True
    )
    updated = jnp.einsum(
        "inc,ijn->jnc", incoming_pieces, trans_w, preferred_element_type=jnp.float32
    ).astype(jnp.bfloat16)
    return lax.all_to_all(updated, "member", split_axis=0, concat_axis=1, tiled=True)


def solution(mesh):
    return jax.shard_map(
        per_device,
        mesh=mesh,
        in_specs=(
            P("member", ("region", "space"), None),
            P("member", ("region", "space")),
            P(("region", "space")),
            P(("region", "space")),
            P(("region", "space"), None),
            P(("region", "space")),
        ),
        out_specs=P("member", ("region", "space"), None),
        check_vma=False,
    )
```

profile of v0, /device:TPU:0, one launch (start us, length us, event | category | flops | bytes accessed | tf_op | source)
XLA Modules:
  0.0 223.0 jit_solution(4702585472627936783)
XLA Ops:
  0.0 15.8 %all-gather = bf16[8,10,384]{2,1,0:T(8,128)(2,1)S(1)} all-gather(bf16[1,10,384]{2,1,0:T(8,128)(2,1)} %bitcast.124), channel_id=1, replica_groups=mesh['region'=2,'member'=8,'space'=2] {'member'}, dimensions={0}, use_global_device_ids=true | all-gather | bytes 69120 | tf_op jit(solution)/shard_map/all_gather | solution.py:88
  15.9 0.1 copy.66
  16.0 0.8 stack.8
  16.8 0.8 stack.9
  17.6 0.1 pad_maximum_fusion.1
  17.7 3.4 %collective-permute-start = (bf16[82,320]{0,1:T(8,128)(2,1)S(1)}, bf16[82,320]{0,1:T(8,128)(2,1)S(1)}, u32[]{:S(2)}, u32[]{:S(2)}) collective-permute-start(bf16[82,320]{0,1:T(8,128)(2,1)S(1)} %get-tuple-element.14), channel_id=1, source_target_pairs={{0,1},{2,3},{4,5},{6,7},{8,9},{10,11},{12,13},{14,15},{16,17},{18,... | collective-permute-start | bytes 157448 | tf_op jit(solution)/shard_map/ppermute | solution.py:16
  21.1 1.3 collective-permute-start.1
  22.4 4.5 %copy.84 = bf16[10,384,256]{2,0,1:T(8,128)(2,1)} copy(bf16[10,384,256]{2,1,0:T(8,128)(2,1)} %param.6) | data formatting | bytes 3932160 | tf_op args[0]
  26.9 4.7 %all-to-all-start = ((bf16[10,384,256]{2,0,1:T(8,128)(2,1)}), bf16[10,384,256]{2,0,1:T(8,128)(2,1)}, u32[]{:S(2)}, u32[]{:S(2)}) async-start(bf16[10,384,256]{2,0,1:T(8,128)(2,1)} %copy.84), calls=%async_computation | async-start | bytes 6291456 | tf_op jit(solution)/shard_map/all_to_all | solution.py:102
  31.6 0.8 compare_and_fusion
  32.4 0.8 add_multiply_fusion
  33.2 0.0 collective-permute-done
  33.2 0.0 collective-permute-done.1
  33.2 0.1 pad_maximum_fusion
  33.3 18.1 %gather_fusion = bf16[6144,82]{1,0:T(8,128)(2,1)S(1)} fusion(bf16[82,1024]{0,1:T(8,128)(2,1)S(1)} %pad_maximum_fusion, s32[6144]{0:T(1024)S(1)} %broadcast_clamp_fusion), kind=kCustom, calls=%fused_computation | custom fusion | bytes 2039808 | tf_op jit(solution)/shard_map/jit(_take)/gather | solution.py:66
  51.4 0.9 copy.69
  52.4 0.1 select_convert_fusion
  52.5 0.2 slice_reduce_fusion
  52.7 0.1 fusion.69
  52.8 1.8 multiply_reduce_fusion
  54.5 0.2 multiply_reduce_fusion.1
  54.7 0.6 fusion.70
  56.0 56.4 %all-reduce = (f32[]{:T(128)}, f32[]{:T(128)}) all-reduce(f32[]{:T(128)S(6)} %div.56, f32[]{:T(128)} %get-tuple-element.5), channel_id=1, replica_groups=mesh['region'=2,'member'=8,'space'=2] {'member','space'}, use_global_device_ids=true, to_apply=%region_3.4 | all-reduce | flops 2 | bytes 16 | tf_op jit(solution)/shard_map/psum | solution.py:99
  113.7 7.0 %abs_reduce_fusion = (f32[80,48]{0,1:T(8,128)S(1)}, f32[48,80,80]{2,1,0:T(8,128)}) fusion(f32[80,80]{0,1:T(8,128)S(1)} %fusion.65, f32[80,48,128]{2,1,0:T(8,128)} %get-tuple-element.10, f32[80,48,128]{2,1,0:T(8,128)S(1)} %get-tuple-element.11), kind=kOutput, calls=%fused_computation.40 | convolution fusion | flops 472776960 | bytes 5201920 | tf_op jit(solution)/shard_map/ank,bnk->abn/dot_general | solution.py:42
  120.7 0.1 reduce_max.9
  120.8 3.6 %fusion.61 = f32[48,80,80]{2,1,0:T(8,128)S(1)} fusion(f32[80,80]{0,1:T(8,128)S(1)} %fusion.67, f32[48,80,80]{2,1,0:T(8,128)} %get-tuple-element.17, f32[48]{0:T(128)S(1)} %reduce_max.9, f32[80,80]{0,1:T(8,128)S(1)} %fusion.65), kind=kOutput, calls=%fused_computation.71 | convolution fusion | flops 295526400 | bytes 2508992 | tf_op jit(solution)/shard_map/abn,bcn->acn/dot_general | solution.py:49
  124.4 0.0 copy-start.2
  124.4 1.8 fusion.34
  126.2 0.0 copy-done.2
  126.2 2.4 %fusion.33 = f32[48,80,80]{2,1,0:T(8,128)S(1)} fusion(f32[48,80,80]{2,1,0:T(8,128)S(1)} %fusion.61, f32[80,80]{0,1:T(8,128)S(1)} %fusion.66, f32[48,80,80]{2,1,0:T(8,128)S(1)} %copy-done.2, f32[48]{0:T(128)S(1)} %reduce_max.9, f32[80,80]{0,1:T(8,128)S(1)} %fusion.65), kind=kOutput, calls=%fused_computation.45 | convolution fusion | flops 296140800 | bytes 3737792 | tf_op jit(solution)/shard_map/abn,bcn->acn/dot_general | solution.py:52
  128.6 0.0 copy-start.1
  128.6 2.4 %fusion.19 = f32[48,80,80]{2,1,0:T(8,128)S(1)} fusion(f32[48,80,80]{2,1,0:T(8,128)S(1)} %fusion.33, f32[48,80,80]{2,1,0:T(8,128)S(1)} %fusion.34), kind=kOutput, calls=%fused_computation.24 | convolution fusion | flops 294912000 | bytes 3686400 | tf_op jit(solution)/shard_map/abn,bcn->acn/dot_general | solution.py:49
  131.0 0.0 copy-done.1
  131.0 0.0 copy-start
  131.1 2.2 fusion.21
  133.2 0.0 copy-done
  133.3 0.1 copy.103
  133.3 4.3 %fusion.17 = f32[48,80,80]{2,1,0:T(8,128)S(1)} fusion(f32[48,80,80]{2,1,0:T(8,128)} %copy-done.1, f32[48,80,80]{2,1,0:T(8,128)} %copy-done, f32[80,80]{0,1:T(8,128)S(1)} %fusion.66), kind=kOutput, calls=%fused_computation.22 | convolution fusion | flops 295526400 | bytes 3712000 | tf_op jit(solution)/shard_map/abn,bcn->acn/dot_general | solution.py:52
  137.7 2.2 fusion.12
  139.9 2.3 %fusion.14 = f32[48,80,80]{2,1,0:T(8,128)S(1)} fusion(f32[48,80,80]{2,1,0:T(8,128)S(1)} %fusion.21, f32[48,80,80]{2,1,0:T(8,128)S(1)} %fusion.12, f32[80,80]{0,1:T(8,128)S(1)} %fusion.66), kind=kOutput, calls=%fused_computation.18 | convolution fusion | flops 295526400 | bytes 3712000 | tf_op jit(solution)/shard_map/abn,bcn->acn/dot_general | solution.py:53
  142.1 2.5 %fusion.10 = f32[48,80,80]{2,1,0:T(8,128)S(1)} fusion(f32[48,80,80]{2,1,0:T(8,128)S(1)} %fusion.17, f32[48,80,80]{2,1,0:T(8,128)S(1)} %fusion.12, f32[80,80]{0,1:T(8,128)S(1)} %fusion.66), kind=kOutput, calls=%fused_computation.14 | convolution fusion | flops 295526400 | bytes 3712000 | tf_op jit(solution)/shard_map/abn,bcn->acn/dot_general | solution.py:52
  144.7 2.2 fusion.6
  146.9 3.5 %fusion.36 = f32[48,80,80]{1,2,0:T(8,128)S(1)} fusion(f32[48,80,80]{2,1,0:T(8,128)S(1)} %fusion.6, f32[48,80,80]{2,1,0:T(8,128)S(1)} %fusion.14, f32[48]{0:T(128)S(1)} %sqrt.7, f32[80,80]{0,1:T(8,128)S(1)} %fusion.66), kind=kOutput, calls=%fused_computation.48 | convolution fusion | flops 295833600 | bytes 3712192 | tf_op jit(solution)/shard_map/abn,bcn->acn/dot_general | solution.py:53
  150.4 3.2 %fusion.39 = f32[80,48,1]{0,2,1:T(1,128)S(1)} fusion(f32[80,48,1]{0,2,1:T(1,128)S(1)} %copy.103, f32[48,80,80]{1,2,0:T(8,128)S(1)} %fusion.36), kind=kOutput, calls=%fused_computation.49 | convolution fusion | flops 3686400 | bytes 1259520 | tf_op jit(solution)/shard_map/abn,bn->an/dot_general | solution.py:56
  153.5 3.2 %fusion = f32[48,1,80]{2,1,0:T(1,128)S(1)} fusion(f32[80,48,1]{0,2,1:T(1,128)S(1)} %fusion.39, f32[48,80,80]{1,2,0:T(8,128)S(1)} %fusion.36), kind=kOutput, calls=%fused_computation.1 | convolution fusion | flops 3686400 | bytes 1259520 | tf_op jit(solution)/shard_map/abn,bn->an/dot_general | solution.py:57
  156.7 0.6 fusion.35
  157.3 0.0 all-to-all-done
  157.3 2.6 %copy.86 = bf16[8,10,48,256]{3,2,1,0:T(8,128)(2,1)S(1)} copy(bf16[8,10,48,256]{3,1,2,0:T(8,128)(2,1)} %bitcast.32) | data formatting | bytes 3932160 | tf_op jit(solution)/shard_map/all_to_all | solution.py:102
  160.0 2.3 %convert_bitcast_fusion = bf16[80,48,256]{2,0,1:T(8,128)(2,1)S(1)} fusion(bf16[80,48,256]{2,1,0:T(8,128)(2,1)S(1)} %bitcast.116, f32[48,80,80]{1,2,0:T(8,128)S(1)} %fusion.36, f32[80,48]{0,1:T(8,128)S(1)} %broadcast_multiply_fusion.1, f32[80,48]{0,1:T(8,128)S(1)} %bitcast.120), kind=kOutput, calls=%fused_computation.36 | convolution fusion | flops 159805440 | bytes 5191680 | tf_op jit(solution)/shard_map/inc,ijn->jnc/dot_general | solution.py:105
  162.3 0.7 copy.89
  162.9 58.4 %all_to_all.36 = bf16[80,48,256]{2,1,0:T(8,128)(2,1)S(1)} all-to-all(bf16[80,48,256]{2,1,0:T(8,128)(2,1)S(1)} %copy.89), channel_id=1, replica_groups=mesh['region'=2,'member'=8,'space'=2] {'member'}, dimensions={0} | all-to-all | bytes 3932160 | tf_op jit(solution)/shard_map/all_to_all | solution.py:108
  221.3 1.5 copy.90
  (11 shorter events, 0.1 us)
Async XLA Ops:
  17.7 15.5 %collective-permute-start = (bf16[82,320]{0,1:T(8,128)(2,1)S(1)}, bf16[82,320]{0,1:T(8,128)(2,1)S(1)}, u32[]{:S(2)}, u32[]{:S(2)}) collective-permute-start(bf16[82,320]{0,1:T(8,128)(2,1)S(1)} %get-tuple-element.14), channel_id=1, source_target_pairs={{0,1},{2,3},{4,5},{6,7},{8,9},{10,11},{12,13},{14,15},{16,17},{18,... | collective-permute-start | bytes 157448 | tf_op jit(solution)/shard_map/ppermute | solution.py:16
  21.1 12.1 %collective-permute-start.1 = (bf16[82,320]{0,1:T(8,128)(2,1)S(1)}, bf16[82,320]{0,1:T(8,128)(2,1)S(1)}, u32[]{:S(2)}, u32[]{:S(2)}) collective-permute-start(bf16[82,320]{0,1:T(8,128)(2,1)S(1)} %get-tuple-element.15), channel_id=1, source_target_pairs={{1,0},{3,2},{5,4},{7,6},{9,8},{11,10},{13,12},{15,14},{17,16},{19,... | collective-permute-start | bytes 157448 | tf_op jit(solution)/shard_map/ppermute | solution.py:17
  26.9 130.4 %all-to-all-start = ((bf16[10,384,256]{2,0,1:T(8,128)(2,1)}), bf16[10,384,256]{2,0,1:T(8,128)(2,1)}, u32[]{:S(2)}, u32[]{:S(2)}) async-start(bf16[10,384,256]{2,0,1:T(8,128)(2,1)} %copy.84), calls=%async_computation | async-start | bytes 6291456 | tf_op jit(solution)/shard_map/all_to_all | solution.py:102
  124.4 1.8 copy-start.2
  128.6 2.4 %copy-start.1 = (f32[48,80,80]{2,1,0:T(8,128)}, f32[48,80,80]{2,1,0:T(8,128)S(1)}, u32[]{:S(2)}) copy-start(f32[48,80,80]{2,1,0:T(8,128)S(1)} %fusion.33) | copy-start | bytes 3686404
  131.0 2.2 copy-start
where the time goes:
time: 227 us; the launch traced here: 223 us
  blocking collectives  131 us (58%)
  matrix products  45 us (20%)
  local copies, waits for them, and re-layouts  30.1 us (13%)
  starting transfers between devices  9.35 us (4%)
  other arithmetic  5.51 us (2%)
  between operations  2.5 us (1%)
    all_to_all x1, blocking collectives, per_device(): lax.all_to_all(updated, 'member', split_axis=0, concat_axis=1, tiled=True)  58.4 us
    psum x1, blocking collectives, per_device(): fit_sum, spread = lax.psum((fit_sum, spread), ('member', 'space'))  56.4 us
    gather x2, local copies, waits for them, and re-layouts, select_domains(): jnp.take(window, obs_lists.reshape(-1), axis=1)  19 us
    all_gather x1, blocking collectives, per_device(): gathered = lax.all_gather(prior_at_sensors, 'member', axis=0, tiled=True)  15.8 us
    dot_general x4, matrix products, transform(): jnp.einsum('abn,bcn->acn', inverse, root_iter, precision=exact)  10.4 us
    dot_general x4, matrix products, transform(): inverse = jnp.einsum('abn,bcn->acn', factor, inverse, precision=exact)  9.78 us
    dot_general x3, matrix products, transform(): root_iter = jnp.einsum('abn,bcn->acn', root_iter, factor, precision=exact)  9.26 us
    dot_general x1, matrix products, transform(): gram = jnp.einsum('ank,bnk->abn', weighted, anomaly, precision=exact)  7.01 us
  transfers between devices with their start and end apart: 3, of which 0 were waited for; matrix products, arithmetic and copies ran while one was open for 32% of the time, Pallas kernels for 0%

commit v1 on v0

--- a/solution.py
+++ b/solution.py
@@ -1,9 +1,27 @@
+import functools
 import jax
 import jax.numpy as jnp
 from jax import lax
 from jax.sharding import PartitionSpec as P
+from jax.lax import all_to_all, axis_size
 
 NS_STEPS = 4
+
+
+def _test_lines(base_x, shard_axis, d_out, axis_k):
+    parts_out = jnp.concatenate(
+        all_to_all(
+            jnp.stack(jnp.split(base_x, axis_size(shard_axis), axis=d_out)),
+            shard_axis,
+            split_axis=0,
+            concat_axis=0,
+        ),
+        axis_k,
+    )
+    return parts_out
+
+
+track_the_matrix = functools.partial(_test_lines, shard_axis="member", d_out=0, axis_k=1)
 
 
 def padded(value, sides, width):
@@ -105,7 +123,7 @@
     updated = jnp.einsum(
         "inc,ijn->jnc", incoming_pieces, trans_w, preferred_element_type=jnp.float32
     ).astype(jnp.bfloat16)
-    return lax.all_to_all(updated, "member", split_axis=0, concat_axis=1, tiled=True)
+    return track_the_matrix(updated)
 
 
 def solution(mesh):

time: 227 us -> 229 us (level)
    unnamed x9 -> x16, local copies, waits for them, and re-layouts: 4.63 us -> 5.38 us
where the time goes in v1:
time: 229 us; the launch traced here: 224 us
  blocking collectives  131 us (57%)
  matrix products  45 us (20%)
  local copies, waits for them, and re-layouts  31.3 us (14%)
  starting transfers between devices  9.35 us (4%)
  other arithmetic  5.51 us (2%)
  between operations  2.59 us (1%)
    all_to_all x1, blocking collectives, _test_lines(): all_to_all(jnp.stack(jnp.split(base_x, axis_size(shard_axis), axis=d_out)...  58.4 us
    psum x1, blocking collectives, per_device(): fit_sum, spread = lax.psum((fit_sum, spread), ('member', 'space'))  56.4 us
    gather x2, local copies, waits for them, and re-layouts, select_domains(): jnp.take(window, obs_lists.reshape(-1), axis=1)  19 us
    all_gather x1, blocking collectives, per_device(): gathered = lax.all_gather(prior_at_sensors, 'member', axis=0, tiled=True)  15.8 us
    dot_general x4, matrix products, transform(): jnp.einsum('abn,bcn->acn', inverse, root_iter, precision=exact)  10.4 us
    dot_general x4, matrix products, transform(): inverse = jnp.einsum('abn,bcn->acn', factor, inverse, precision=exact)  9.78 us
    dot_general x3, matrix products, transform(): root_iter = jnp.einsum('abn,bcn->acn', root_iter, factor, precision=exact)  9.26 us
    dot_general x1, matrix products, transform(): gram = jnp.einsum('ank,bnk->abn', weighted, anomaly, precision=exact)  7.01 us
  transfers between devices with their start and end apart: 3, of which 0 were waited for; matrix products, arithmetic and copies ran while one was open for 32% of the time, Pallas kernels for 0%

profile of v1, /device:TPU:0, one launch (start us, length us, event | category | flops | bytes accessed | tf_op | source)
XLA Modules:
  0.0 224.3 jit_solution(8232275140895990626)
XLA Ops:
  0.0 15.8 %all-gather = bf16[8,10,384]{2,1,0:T(8,128)(2,1)S(1)} all-gather(bf16[1,10,384]{2,1,0:T(8,128)(2,1)} %bitcast.154), channel_id=1, replica_groups=mesh['region'=2,'member'=8,'space'=2] {'member'}, dimensions={0}, use_global_device_ids=true | all-gather | bytes 69120 | tf_op jit(solution)/shard_map/all_gather | solution.py:106
  15.9 0.1 copy.89
  16.0 0.8 stack.44
  16.8 0.8 stack.45
  17.6 0.1 pad_maximum_fusion.1
  17.7 3.4 %collective-permute-start = (bf16[82,320]{0,1:T(8,128)(2,1)S(1)}, bf16[82,320]{0,1:T(8,128)(2,1)S(1)}, u32[]{:S(2)}, u32[]{:S(2)}) collective-permute-start(bf16[82,320]{0,1:T(8,128)(2,1)S(1)} %get-tuple-element.14), channel_id=1, source_target_pairs={{0,1},{2,3},{4,5},{6,7},{8,9},{10,11},{12,13},{14,15},{16,17},{18,... | collective-permute-start | bytes 157448 | tf_op jit(solution)/shard_map/ppermute | solution.py:34
  21.1 1.3 collective-permute-start.1
  22.4 4.5 %copy.107 = bf16[10,384,256]{2,0,1:T(8,128)(2,1)} copy(bf16[10,384,256]{2,1,0:T(8,128)(2,1)} %param.6) | data formatting | bytes 3932160 | tf_op args[0]
  26.9 4.7 %all-to-all-start = ((bf16[10,384,256]{2,0,1:T(8,128)(2,1)}), bf16[10,384,256]{2,0,1:T(8,128)(2,1)}, u32[]{:S(2)}, u32[]{:S(2)}) async-start(bf16[10,384,256]{2,0,1:T(8,128)(2,1)} %copy.107), calls=%async_computation | async-start | bytes 6291456 | tf_op jit(solution)/shard_map/all_to_all | solution.py:120
  31.6 0.8 compare_and_fusion
  32.4 0.8 add_multiply_fusion
  33.2 0.0 collective-permute-done
  33.2 0.0 collective-permute-done.1
  33.2 0.1 pad_maximum_fusion
  33.3 18.1 %gather_fusion = bf16[6144,82]{1,0:T(8,128)(2,1)S(1)} fusion(bf16[82,1024]{0,1:T(8,128)(2,1)S(1)} %pad_maximum_fusion, s32[6144]{0:T(1024)S(1)} %broadcast_clamp_fusion), kind=kCustom, calls=%fused_computation | custom fusion | bytes 2039808 | tf_op jit(solution)/shard_map/jit(_take)/gather | solution.py:84
  51.4 0.9 copy.92
  52.4 0.1 select_convert_fusion
  52.5 0.2 slice_reduce_fusion
  52.7 0.1 fusion.77
  52.8 1.8 multiply_reduce_fusion
  54.5 0.2 multiply_reduce_fusion.1
  54.7 0.6 fusion.78
  56.0 56.4 %all-reduce = (f32[]{:T(128)}, f32[]{:T(128)}) all-reduce(f32[]{:T(128)S(6)} %div.56, f32[]{:T(128)} %get-tuple-element.5), channel_id=1, replica_groups=mesh['region'=2,'member'=8,'space'=2] {'member','space'}, use_global_device_ids=true, to_apply=%region_3.4 | all-reduce | flops 2 | bytes 16 | tf_op jit(solution)/shard_map/psum | solution.py:117
  113.7 7.0 %abs_reduce_fusion = (f32[80,48]{0,1:T(8,128)S(1)}, f32[48,80,80]{2,1,0:T(8,128)}) fusion(f32[80,80]{0,1:T(8,128)S(1)} %fusion.73, f32[80,48,128]{2,1,0:T(8,128)} %get-tuple-element.10, f32[80,48,128]{2,1,0:T(8,128)S(1)} %get-tuple-element.11), kind=kOutput, calls=%fused_computation.40 | convolution fusion | flops 472776960 | bytes 5201920 | tf_op jit(solution)/shard_map/ank,bnk->abn/dot_general | solution.py:60
  120.7 0.1 reduce_max.9
  120.8 3.6 %fusion.61 = f32[48,80,80]{2,1,0:T(8,128)S(1)} fusion(f32[80,80]{0,1:T(8,128)S(1)} %fusion.75, f32[48,80,80]{2,1,0:T(8,128)} %get-tuple-element.17, f32[48]{0:T(128)S(1)} %reduce_max.9, f32[80,80]{0,1:T(8,128)S(1)} %fusion.73), kind=kOutput, calls=%fused_computation.71 | convolution fusion | flops 295526400 | bytes 2508992 | tf_op jit(solution)/shard_map/abn,bcn->acn/dot_general | solution.py:67
  124.4 0.0 copy-start.2
  124.4 1.8 fusion.34
  126.2 0.0 copy-done.2
  126.2 2.4 %fusion.33 = f32[48,80,80]{2,1,0:T(8,128)S(1)} fusion(f32[48,80,80]{2,1,0:T(8,128)S(1)} %fusion.61, f32[80,80]{0,1:T(8,128)S(1)} %fusion.74, f32[48,80,80]{2,1,0:T(8,128)S(1)} %copy-done.2, f32[48]{0:T(128)S(1)} %reduce_max.9, f32[80,80]{0,1:T(8,128)S(1)} %fusion.73), kind=kOutput, calls=%fused_computation.45 | convolution fusion | flops 296140800 | bytes 3737792 | tf_op jit(solution)/shard_map/abn,bcn->acn/dot_general | solution.py:70
  128.6 0.0 copy-start.1
  128.6 2.4 %fusion.19 = f32[48,80,80]{2,1,0:T(8,128)S(1)} fusion(f32[48,80,80]{2,1,0:T(8,128)S(1)} %fusion.33, f32[48,80,80]{2,1,0:T(8,128)S(1)} %fusion.34), kind=kOutput, calls=%fused_computation.24 | convolution fusion | flops 294912000 | bytes 3686400 | tf_op jit(solution)/shard_map/abn,bcn->acn/dot_general | solution.py:67
  131.0 0.0 copy-done.1
  131.0 0.0 copy-start
  131.0 2.2 fusion.21
  133.2 0.0 copy-done
  133.3 0.1 copy.126
  133.3 4.3 %fusion.17 = f32[48,80,80]{2,1,0:T(8,128)S(1)} fusion(f32[48,80,80]{2,1,0:T(8,128)} %copy-done.1, f32[48,80,80]{2,1,0:T(8,128)} %copy-done, f32[80,80]{0,1:T(8,128)S(1)} %fusion.74), kind=kOutput, calls=%fused_computation.22 | convolution fusion | flops 295526400 | bytes 3712000 | tf_op jit(solution)/shard_map/abn,bcn->acn/dot_general | solution.py:70
  137.7 2.2 fusion.12
  139.8 2.3 %fusion.14 = f32[48,80,80]{2,1,0:T(8,128)S(1)} fusion(f32[48,80,80]{2,1,0:T(8,128)S(1)} %fusion.21, f32[48,80,80]{2,1,0:T(8,128)S(1)} %fusion.12, f32[80,80]{0,1:T(8,128)S(1)} %fusion.74), kind=kOutput, calls=%fused_computation.18 | convolution fusion | flops 295526400 | bytes 3712000 | tf_op jit(solution)/shard_map/abn,bcn->acn/dot_general | solution.py:71
  142.1 2.5 %fusion.10 = f32[48,80,80]{2,1,0:T(8,128)S(1)} fusion(f32[48,80,80]{2,1,0:T(8,128)S(1)} %fusion.17, f32[48,80,80]{2,1,0:T(8,128)S(1)} %fusion.12, f32[80,80]{0,1:T(8,128)S(1)} %fusion.74), kind=kOutput, calls=%fused_computation.14 | convolution fusion | flops 295526400 | bytes 3712000 | tf_op jit(solution)/shard_map/abn,bcn->acn/dot_general | solution.py:70
  144.7 2.2 fusion.6
  146.9 3.5 %fusion.36 = f32[48,80,80]{1,2,0:T(8,128)S(1)} fusion(f32[48,80,80]{2,1,0:T(8,128)S(1)} %fusion.6, f32[48,80,80]{2,1,0:T(8,128)S(1)} %fusion.14, f32[48]{0:T(128)S(1)} %sqrt.7, f32[80,80]{0,1:T(8,128)S(1)} %fusion.74), kind=kOutput, calls=%fused_computation.48 | convolution fusion | flops 295833600 | bytes 3712192 | tf_op jit(solution)/shard_map/abn,bcn->acn/dot_general | solution.py:71
  150.4 3.2 %fusion.39 = f32[80,48,1]{0,2,1:T(1,128)S(1)} fusion(f32[80,48,1]{0,2,1:T(1,128)S(1)} %copy.126, f32[48,80,80]{1,2,0:T(8,128)S(1)} %fusion.36), kind=kOutput, calls=%fused_computation.49 | convolution fusion | flops 3686400 | bytes 1259520 | tf_op jit(solution)/shard_map/abn,bn->an/dot_general | solution.py:74
  153.5 3.2 %fusion = f32[48,1,80]{2,1,0:T(1,128)S(1)} fusion(f32[80,48,1]{0,2,1:T(1,128)S(1)} %fusion.39, f32[48,80,80]{1,2,0:T(8,128)S(1)} %fusion.36), kind=kOutput, calls=%fused_computation.1 | convolution fusion | flops 3686400 | bytes 1259520 | tf_op jit(solution)/shard_map/abn,bn->an/dot_general | solution.py:75
  156.7 0.6 fusion.35
  157.3 0.0 all-to-all-done
  157.3 2.9 %copy.109 = bf16[8,10,48,256]{3,2,1,0:T(8,128)(2,1)S(1)} copy(bf16[8,10,48,256]{3,1,2,0:T(8,128)(2,1)} %bitcast.32) | data formatting | bytes 3932160 | tf_op jit(solution)/shard_map/all_to_all | solution.py:120
  160.2 2.3 %convert_bitcast_fusion = bf16[80,48,256]{2,0,1:T(8,128)(2,1)S(1)} fusion(bf16[80,48,256]{2,1,0:T(8,128)(2,1)S(1)} %bitcast.147, f32[48,80,80]{1,2,0:T(8,128)S(1)} %fusion.36, f32[80,48]{0,1:T(8,128)S(1)} %broadcast_multiply_fusion.1, f32[80,48]{0,1:T(8,128)S(1)} %bitcast.150), kind=kOutput, calls=%fused_computation.36 | convolution fusion | flops 159805440 | bytes 5191680 | tf_op jit(solution)/shard_map/inc,ijn->jnc/dot_general | solution.py:123
  162.6 0.1 fusion.69
  162.7 0.1 fusion.68
  162.8 0.1 fusion.67
  163.0 0.1 fusion.65
  163.2 0.1 fusion.64
  163.3 0.1 fusion.63
  163.4 0.8 copy.112
  164.2 58.4 %all_to_all.23 = bf16[8,10,48,256]{3,2,1,0:T(8,128)(2,1)S(1)} all-to-all(bf16[8,10,48,256]{3,2,1,0:T(8,128)(2,1)S(1)} %copy.112), channel_id=1, replica_groups=mesh['region'=2,'member'=8,'space'=2] {'member'}, dimensions={0} | all-to-all | bytes 3932160 | tf_op jit(solution)/shard_map/all_to_all | solution.py:13
  222.6 1.5 copy.113
  (13 shorter events, 0.2 us)
Async XLA Ops:
  17.7 15.5 %collective-permute-start = (bf16[82,320]{0,1:T(8,128)(2,1)S(1)}, bf16[82,320]{0,1:T(8,128)(2,1)S(1)}, u32[]{:S(2)}, u32[]{:S(2)}) collective-permute-start(bf16[82,320]{0,1:T(8,128)(2,1)S(1)} %get-tuple-element.14), channel_id=1, source_target_pairs={{0,1},{2,3},{4,5},{6,7},{8,9},{10,11},{12,13},{14,15},{16,17},{18,... | collective-permute-start | bytes 157448 | tf_op jit(solution)/shard_map/ppermute | solution.py:34
  21.1 12.1 %collective-permute-start.1 = (bf16[82,320]{0,1:T(8,128)(2,1)S(1)}, bf16[82,320]{0,1:T(8,128)(2,1)S(1)}, u32[]{:S(2)}, u32[]{:S(2)}) collective-permute-start(bf16[82,320]{0,1:T(8,128)(2,1)S(1)} %get-tuple-element.15), channel_id=1, source_target_pairs={{1,0},{3,2},{5,4},{7,6},{9,8},{11,10},{13,12},{15,14},{17,16},{19,... | collective-permute-start | bytes 157448 | tf_op jit(solution)/shard_map/ppermute | solution.py:35
  26.9 130.4 %all-to-all-start = ((bf16[10,384,256]{2,0,1:T(8,128)(2,1)}), bf16[10,384,256]{2,0,1:T(8,128)(2,1)}, u32[]{:S(2)}, u32[]{:S(2)}) async-start(bf16[10,384,256]{2,0,1:T(8,128)(2,1)} %copy.107), calls=%async_computation | async-start | bytes 6291456 | tf_op jit(solution)/shard_map/all_to_all | solution.py:120
  124.4 1.8 copy-start.2
  128.6 2.4 %copy-start.1 = (f32[48,80,80]{2,1,0:T(8,128)}, f32[48,80,80]{2,1,0:T(8,128)S(1)}, u32[]{:S(2)}) copy-start(f32[48,80,80]{2,1,0:T(8,128)S(1)} %fusion.33) | copy-start | bytes 3686404
  131.0 2.2 copy-start
